TPU v7x, 256 devices: a whole 4x4x8 slice. The times are simulated.
256 devices in a mesh: rad: 32 (over x, y, core), pol: 8 (over z).
Axes of the slice: x: 4, y: 4, z: 8, core: 2. Of those that a mesh axis runs over, the one named last changes fastest.
Arguments:
- dust: float32 [128, 64, 16384], P(None, 'pol', 'rad'), may hold values from 0.2 to 2
- drift_courant: float32 [128], replicated, may hold values from 0.1 to 0.6
- mixing: float32 [128], replicated, may hold values from 0.02 to 0.1
- pair_table: int32 [3, 2048], replicated, may hold values from 0 to 127
- pair_rate: float32 [2048], replicated, may hold values from 0.002 to 0.02
- absorption: float32 [128, 128], replicated, may hold values from 0.05 to 5
- stellar_flux: float32 [128], replicated, may hold values from 0.01 to 0.1
- band_channel: int32 [128], replicated, may hold values from 0 to 3
Outputs:
- new_dust: float32 [128, 64, 16384], P(None, 'pol', 'rad')
- heating: float32 [4, 64, 16384], P(None, 'pol', 'rad')
Inputs may be any that keep to these rules, and one draw needn't show every extreme that they name: `pair_table`: sizes of dust.
All inputs are finite; a program needn't handle non-finite values.
Results may differ from a plain program's by a relative error of at most 0.00005.
Values sent between devices are 32-bit elements; how exact they have to be, the bound alone decides.
A program may use at most 192 MiB of HBM per device.

v0:
```python
import jax
import jax.numpy as jnp
from jax import lax
from jax.sharding import PartitionSpec as P

CH = 4
depth_scale = 4.0


def padded_2(cells, sides, width):
    for axis, dim in sides:
        count = lax.axis_size(axis)
        ends = count - 1
        head = lax.slice_in_dim(cells, 0, width, axis=dim)
        tail = lax.slice_in_dim(cells, cells.shape[dim] - width, cells.shape[dim], axis=dim)
        cells = jnp.concatenate(
            [
                lax.ppermute(tail, axis, [(i, (i + 1) % count) for i in range(ends)]),
                cells,
                lax.ppermute(head, axis, [((i + 1) % count, i) for i in range(ends)]),
            ],
            axis=dim,
        )
    return cells


def collide(advected, pair_table, pair_rate):
    sizes = advected.shape[0]
    grid = jnp.arange(sizes, dtype=jnp.int32)
    first = pair_table[0]
    second = pair_table[1]
    target = pair_table[2]
    pick_first = (first[:, None] == grid[None, :]).astype(jnp.float32)
    pick_second = (second[:, None] == grid[None, :]).astype(jnp.float32)
    redistribute = (grid[:, None] == target[None, :]).astype(jnp.float32)
    redistribute = redistribute - (grid[:, None] == first[None, :]).astype(jnp.float32)
    redistribute = redistribute - (grid[:, None] == second[None, :]).astype(jnp.float32)

    def one_row(column):
        left_part = jnp.dot(
            pick_first, column, precision=lax.Precision.HIGHEST, preferred_element_type=jnp.float32
        )
        right_part = jnp.dot(
            pick_second, column, precision=lax.Precision.HIGHEST, preferred_element_type=jnp.float32
        )
        product = pair_rate[:, None] * left_part * right_part
        return column + jnp.dot(
            redistribute,
            product,
            precision=lax.Precision.HIGHEST,
            preferred_element_type=jnp.float32,
        )

    rows = lax.map(one_row, jnp.moveaxis(advected, 1, 0))
    return jnp.moveaxis(rows, 0, 1)


def shards(
    dust, drift_courant, mixing, pair_table, pair_rate, absorption, stellar_flux, band_channel
):
    padded = padded_2(dust, (("rad", 2), ("pol", 1)), 1)
    center = padded[:, 1:-1, 1:-1]
    outer = padded[:, 1:-1, 2:]
    inner = padded[:, 1:-1, :-2]
    upper = padded[:, 2:, 1:-1]
    lower = padded[:, :-2, 1:-1]
    drift = drift_courant[:, None, None]
    spread = mixing[:, None, None]
    advected = (
        center + drift * (outer - center) + spread * (outer + inner + upper + lower - 4.0 * center)
    )
    new_dust = collide(advected, pair_table, pair_rate)
    sizes = absorption.shape[1]
    opacity = (
        jnp.einsum("bs,str->btr", absorption, new_dust, precision=lax.Precision.HIGHEST) / sizes
    )
    tile = dust.shape[2]
    rad_count = lax.axis_size("rad")
    ray_length = tile * rad_count
    cell_index = jnp.arange(tile, dtype=jnp.int32)
    strict_upper = (cell_index[:, None] < cell_index[None, :]).astype(jnp.float32)
    channels = jnp.arange(CH, dtype=jnp.int32)
    ray_block = lax.all_to_all(opacity, "rad", split_axis=0, concat_axis=2, tiled=True)
    local_bands = ray_block.shape[0]
    polar_rows = ray_block.shape[1]
    first_band = lax.axis_index("rad") * local_bands
    step_depth = ray_block * (depth_scale / ray_length)
    pieces = step_depth.reshape(local_bands, polar_rows, rad_count, tile)
    within = jnp.einsum("bkni,ij->bknj", pieces, strict_upper, precision=lax.Precision.HIGHEST)
    totals = jnp.sum(pieces, axis=3)
    offsets = jnp.cumsum(totals, axis=2) - totals
    depth = (within + offsets[..., None]).reshape(step_depth.shape)
    flux_part = lax.dynamic_slice_in_dim(stellar_flux, first_band, local_bands)
    channel_part = lax.dynamic_slice_in_dim(band_channel, first_band, local_bands)
    absorbed = flux_part[:, None, None] * jnp.exp(-depth) * -jnp.expm1(-step_depth) * ray_length
    picker = (channels[:, None] == channel_part[None, :]).astype(jnp.float32)
    partial_heat = jnp.einsum("cb,bkr->ckr", picker, absorbed, precision=lax.Precision.HIGHEST)
    heating = lax.psum_scatter(partial_heat, "rad", scatter_dimension=2, tiled=True)
    return (new_dust, heating)


def solution(mesh):
    placed = (P(None, "pol", "rad"), P(), P(), P(), P(), P(), P(), P())
    return jax.shard_map(
        shards,
        mesh=mesh,
        in_specs=placed,
        out_specs=(P(None, "pol", "rad"), P(None, "pol", "rad")),
        check_vma=False,
    )
```

profile of v0, /device:TPU:32, one launch (start us, length us, event | category | flops | bytes accessed | tf_op | source)
XLA Modules:
  0.0 392.9 jit_solution(9531429614701989408)
XLA Ops:
  7.2 2.0 copy.58
  9.3 1.7 collective-permute-start.1
  12.3 3.1 collective-permute-done
  15.5 2.0 collective-permute-start.2
  17.5 3.8 collective-permute-start.3
  21.4 3.7 collective-permute-done.2
  25.1 2.3 collective-permute-done.3
  27.4 3.2 fusion.46
  30.5 118.0 %while.12 = (s32[]{:T(128)}, f32[8,128,512]{1,2,0:T(8,128)}, f32[8,128,512]{1,2,0:T(8,128)}, f32[2048]{0:T(1024)S(1)}, s32[2048]{0:T(1024)S(1)}, /*index=5*/s32[2048]{0:T(1024)S(1)}, s32[2048]{0:T(1024)S(1)}, s32[]{:T(128)}) while((s32[]{:T(128)}, f32[8,128,512]{1,2,0:T(8,128)}, f32[8,128,512]{1,2,0:T(8,128)}, ...), condition=%wide.region_1.2_spmd.clone.clone, body=%wide.region_0.1_spmd.clone.clone.sunk | while | flops 4837146624 | bytes 17875048 | solution.py:54
  30.5 4.6 %fusion.86 = f32[512,2048]{1,0:T(8,128)S(1)} fusion(s32[2048]{0:T(1024)S(1)} %get-tuple-element.184, f32[8,128,512]{1,2,0:T(8,128)} %get-tuple-element.181, s32[]{:T(128)S(6)} %copy.88), kind=kOutput, calls=%fused_computation.19.clone.1 | convolution fusion | flops 1611137024 | bytes 4464644 | tf_op jit(solution)/shard_map/while/body/eval_jaxpr/dot_general | solution.py:43
  35.1 4.6 %fusion.87 = f32[512,2048]{1,0:T(8,128)S(1)} fusion(s32[2048]{0:T(1024)S(1)} %get-tuple-element.183, f32[8,128,512]{1,2,0:T(8,128)} %get-tuple-element.181, s32[]{:T(128)S(6)} %copy.88), kind=kOutput, calls=%fused_computation.22.clone.1 | convolution fusion | flops 1611137024 | bytes 4464644 | tf_op jit(solution)/shard_map/while/body/eval_jaxpr/dot_general | solution.py:40
  39.7 5.6 %fusion.88 = f32[8,128,512]{1,2,0:T(8,128)} fusion(f32[8,128,512]{1,2,0:T(8,128)} %get-tuple-element.172, s32[]{:T(128)S(6)} %copy.88, f32[512,2048]{1,0:T(8,128)S(1)} %fusion.86, f32[512,2048]{1,0:T(8,128)S(1)} %fusion.87, f32[2048]{0:T(1024)S(1)} %get-tuple-element.182, s32[2048]{0:T(1024)S(1)} %get-tuple-element.184, ...), kind=kOutput, calls=%fused_computation.10.clone.1 | convolution fusion | flops 1614872576 | bytes 8945668 | tf_op jit(solution)/shard_map/while/body/eval_jaxpr/dot_general | solution.py:47
  45.3 4.6 %fusion.86 = f32[512,2048]{1,0:T(8,128)S(1)} fusion(s32[2048]{0:T(1024)S(1)} %get-tuple-element.184, f32[8,128,512]{1,2,0:T(8,128)} %get-tuple-element.181, s32[]{:T(128)S(6)} %copy.88), kind=kOutput, calls=%fused_computation.19.clone.1 | convolution fusion | flops 1611137024 | bytes 4464644 | tf_op jit(solution)/shard_map/while/body/eval_jaxpr/dot_general | solution.py:43
  49.9 4.6 %fusion.87 = f32[512,2048]{1,0:T(8,128)S(1)} fusion(s32[2048]{0:T(1024)S(1)} %get-tuple-element.183, f32[8,128,512]{1,2,0:T(8,128)} %get-tuple-element.181, s32[]{:T(128)S(6)} %copy.88), kind=kOutput, calls=%fused_computation.22.clone.1 | convolution fusion | flops 1611137024 | bytes 4464644 | tf_op jit(solution)/shard_map/while/body/eval_jaxpr/dot_general | solution.py:40
  54.5 5.6 %fusion.88 = f32[8,128,512]{1,2,0:T(8,128)} fusion(f32[8,128,512]{1,2,0:T(8,128)} %get-tuple-element.172, s32[]{:T(128)S(6)} %copy.88, f32[512,2048]{1,0:T(8,128)S(1)} %fusion.86, f32[512,2048]{1,0:T(8,128)S(1)} %fusion.87, f32[2048]{0:T(1024)S(1)} %get-tuple-element.182, s32[2048]{0:T(1024)S(1)} %get-tuple-element.184, ...), kind=kOutput, calls=%fused_computation.10.clone.1 | convolution fusion | flops 1614872576 | bytes 8945668 | tf_op jit(solution)/shard_map/while/body/eval_jaxpr/dot_general | solution.py:47
  60.0 4.6 %fusion.86 = f32[512,2048]{1,0:T(8,128)S(1)} fusion(s32[2048]{0:T(1024)S(1)} %get-tuple-element.184, f32[8,128,512]{1,2,0:T(8,128)} %get-tuple-element.181, s32[]{:T(128)S(6)} %copy.88), kind=kOutput, calls=%fused_computation.19.clone.1 | convolution fusion | flops 1611137024 | bytes 4464644 | tf_op jit(solution)/shard_map/while/body/eval_jaxpr/dot_general | solution.py:43
  64.6 4.6 %fusion.87 = f32[512,2048]{1,0:T(8,128)S(1)} fusion(s32[2048]{0:T(1024)S(1)} %get-tuple-element.183, f32[8,128,512]{1,2,0:T(8,128)} %get-tuple-element.181, s32[]{:T(128)S(6)} %copy.88), kind=kOutput, calls=%fused_computation.22.clone.1 | convolution fusion | flops 1611137024 | bytes 4464644 | tf_op jit(solution)/shard_map/while/body/eval_jaxpr/dot_general | solution.py:40
  69.2 5.6 %fusion.88 = f32[8,128,512]{1,2,0:T(8,128)} fusion(f32[8,128,512]{1,2,0:T(8,128)} %get-tuple-element.172, s32[]{:T(128)S(6)} %copy.88, f32[512,2048]{1,0:T(8,128)S(1)} %fusion.86, f32[512,2048]{1,0:T(8,128)S(1)} %fusion.87, f32[2048]{0:T(1024)S(1)} %get-tuple-element.182, s32[2048]{0:T(1024)S(1)} %get-tuple-element.184, ...), kind=kOutput, calls=%fused_computation.10.clone.1 | convolution fusion | flops 1614872576 | bytes 8945668 | tf_op jit(solution)/shard_map/while/body/eval_jaxpr/dot_general | solution.py:47
  74.8 4.6 %fusion.86 = f32[512,2048]{1,0:T(8,128)S(1)} fusion(s32[2048]{0:T(1024)S(1)} %get-tuple-element.184, f32[8,128,512]{1,2,0:T(8,128)} %get-tuple-element.181, s32[]{:T(128)S(6)} %copy.88), kind=kOutput, calls=%fused_computation.19.clone.1 | convolution fusion | flops 1611137024 | bytes 4464644 | tf_op jit(solution)/shard_map/while/body/eval_jaxpr/dot_general | solution.py:43
  79.4 4.6 %fusion.87 = f32[512,2048]{1,0:T(8,128)S(1)} fusion(s32[2048]{0:T(1024)S(1)} %get-tuple-element.183, f32[8,128,512]{1,2,0:T(8,128)} %get-tuple-element.181, s32[]{:T(128)S(6)} %copy.88), kind=kOutput, calls=%fused_computation.22.clone.1 | convolution fusion | flops 1611137024 | bytes 4464644 | tf_op jit(solution)/shard_map/while/body/eval_jaxpr/dot_general | solution.py:40
  84.0 5.6 %fusion.88 = f32[8,128,512]{1,2,0:T(8,128)} fusion(f32[8,128,512]{1,2,0:T(8,128)} %get-tuple-element.172, s32[]{:T(128)S(6)} %copy.88, f32[512,2048]{1,0:T(8,128)S(1)} %fusion.86, f32[512,2048]{1,0:T(8,128)S(1)} %fusion.87, f32[2048]{0:T(1024)S(1)} %get-tuple-element.182, s32[2048]{0:T(1024)S(1)} %get-tuple-element.184, ...), kind=kOutput, calls=%fused_computation.10.clone.1 | convolution fusion | flops 1614872576 | bytes 8945668 | tf_op jit(solution)/shard_map/while/body/eval_jaxpr/dot_general | solution.py:47
  89.5 4.6 %fusion.86 = f32[512,2048]{1,0:T(8,128)S(1)} fusion(s32[2048]{0:T(1024)S(1)} %get-tuple-element.184, f32[8,128,512]{1,2,0:T(8,128)} %get-tuple-element.181, s32[]{:T(128)S(6)} %copy.88), kind=kOutput, calls=%fused_computation.19.clone.1 | convolution fusion | flops 1611137024 | bytes 4464644 | tf_op jit(solution)/shard_map/while/body/eval_jaxpr/dot_general | solution.py:43
  94.1 4.6 %fusion.87 = f32[512,2048]{1,0:T(8,128)S(1)} fusion(s32[2048]{0:T(1024)S(1)} %get-tuple-element.183, f32[8,128,512]{1,2,0:T(8,128)} %get-tuple-element.181, s32[]{:T(128)S(6)} %copy.88), kind=kOutput, calls=%fused_computation.22.clone.1 | convolution fusion | flops 1611137024 | bytes 4464644 | tf_op jit(solution)/shard_map/while/body/eval_jaxpr/dot_general | solution.py:40
  98.7 5.6 %fusion.88 = f32[8,128,512]{1,2,0:T(8,128)} fusion(f32[8,128,512]{1,2,0:T(8,128)} %get-tuple-element.172, s32[]{:T(128)S(6)} %copy.88, f32[512,2048]{1,0:T(8,128)S(1)} %fusion.86, f32[512,2048]{1,0:T(8,128)S(1)} %fusion.87, f32[2048]{0:T(1024)S(1)} %get-tuple-element.182, s32[2048]{0:T(1024)S(1)} %get-tuple-element.184, ...), kind=kOutput, calls=%fused_computation.10.clone.1 | convolution fusion | flops 1614872576 | bytes 8945668 | tf_op jit(solution)/shard_map/while/body/eval_jaxpr/dot_general | solution.py:47
  104.3 4.6 %fusion.86 = f32[512,2048]{1,0:T(8,128)S(1)} fusion(s32[2048]{0:T(1024)S(1)} %get-tuple-element.184, f32[8,128,512]{1,2,0:T(8,128)} %get-tuple-element.181, s32[]{:T(128)S(6)} %copy.88), kind=kOutput, calls=%fused_computation.19.clone.1 | convolution fusion | flops 1611137024 | bytes 4464644 | tf_op jit(solution)/shard_map/while/body/eval_jaxpr/dot_general | solution.py:43
  108.9 4.6 %fusion.87 = f32[512,2048]{1,0:T(8,128)S(1)} fusion(s32[2048]{0:T(1024)S(1)} %get-tuple-element.183, f32[8,128,512]{1,2,0:T(8,128)} %get-tuple-element.181, s32[]{:T(128)S(6)} %copy.88), kind=kOutput, calls=%fused_computation.22.clone.1 | convolution fusion | flops 1611137024 | bytes 4464644 | tf_op jit(solution)/shard_map/while/body/eval_jaxpr/dot_general | solution.py:40
  113.5 5.6 %fusion.88 = f32[8,128,512]{1,2,0:T(8,128)} fusion(f32[8,128,512]{1,2,0:T(8,128)} %get-tuple-element.172, s32[]{:T(128)S(6)} %copy.88, f32[512,2048]{1,0:T(8,128)S(1)} %fusion.86, f32[512,2048]{1,0:T(8,128)S(1)} %fusion.87, f32[2048]{0:T(1024)S(1)} %get-tuple-element.182, s32[2048]{0:T(1024)S(1)} %get-tuple-element.184, ...), kind=kOutput, calls=%fused_computation.10.clone.1 | convolution fusion | flops 1614872576 | bytes 8945668 | tf_op jit(solution)/shard_map/while/body/eval_jaxpr/dot_general | solution.py:47
  119.1 4.6 %fusion.86 = f32[512,2048]{1,0:T(8,128)S(1)} fusion(s32[2048]{0:T(1024)S(1)} %get-tuple-element.184, f32[8,128,512]{1,2,0:T(8,128)} %get-tuple-element.181, s32[]{:T(128)S(6)} %copy.88), kind=kOutput, calls=%fused_computation.19.clone.1 | convolution fusion | flops 1611137024 | bytes 4464644 | tf_op jit(solution)/shard_map/while/body/eval_jaxpr/dot_general | solution.py:43
  123.6 4.6 %fusion.87 = f32[512,2048]{1,0:T(8,128)S(1)} fusion(s32[2048]{0:T(1024)S(1)} %get-tuple-element.183, f32[8,128,512]{1,2,0:T(8,128)} %get-tuple-element.181, s32[]{:T(128)S(6)} %copy.88), kind=kOutput, calls=%fused_computation.22.clone.1 | convolution fusion | flops 1611137024 | bytes 4464644 | tf_op jit(solution)/shard_map/while/body/eval_jaxpr/dot_general | solution.py:40
  128.3 5.6 %fusion.88 = f32[8,128,512]{1,2,0:T(8,128)} fusion(f32[8,128,512]{1,2,0:T(8,128)} %get-tuple-element.172, s32[]{:T(128)S(6)} %copy.88, f32[512,2048]{1,0:T(8,128)S(1)} %fusion.86, f32[512,2048]{1,0:T(8,128)S(1)} %fusion.87, f32[2048]{0:T(1024)S(1)} %get-tuple-element.182, s32[2048]{0:T(1024)S(1)} %get-tuple-element.184, ...), kind=kOutput, calls=%fused_computation.10.clone.1 | convolution fusion | flops 1614872576 | bytes 8945668 | tf_op jit(solution)/shard_map/while/body/eval_jaxpr/dot_general | solution.py:47
  133.8 4.6 %fusion.86 = f32[512,2048]{1,0:T(8,128)S(1)} fusion(s32[2048]{0:T(1024)S(1)} %get-tuple-element.184, f32[8,128,512]{1,2,0:T(8,128)} %get-tuple-element.181, s32[]{:T(128)S(6)} %copy.88), kind=kOutput, calls=%fused_computation.19.clone.1 | convolution fusion | flops 1611137024 | bytes 4464644 | tf_op jit(solution)/shard_map/while/body/eval_jaxpr/dot_general | solution.py:43
  138.4 4.6 %fusion.87 = f32[512,2048]{1,0:T(8,128)S(1)} fusion(s32[2048]{0:T(1024)S(1)} %get-tuple-element.183, f32[8,128,512]{1,2,0:T(8,128)} %get-tuple-element.181, s32[]{:T(128)S(6)} %copy.88), kind=kOutput, calls=%fused_computation.22.clone.1 | convolution fusion | flops 1611137024 | bytes 4464644 | tf_op jit(solution)/shard_map/while/body/eval_jaxpr/dot_general | solution.py:40
  143.0 5.6 %fusion.88 = f32[8,128,512]{1,2,0:T(8,128)} fusion(f32[8,128,512]{1,2,0:T(8,128)} %get-tuple-element.172, s32[]{:T(128)S(6)} %copy.88, f32[512,2048]{1,0:T(8,128)S(1)} %fusion.86, f32[512,2048]{1,0:T(8,128)S(1)} %fusion.87, f32[2048]{0:T(1024)S(1)} %get-tuple-element.182, s32[2048]{0:T(1024)S(1)} %get-tuple-element.184, ...), kind=kOutput, calls=%fused_computation.10.clone.1 | convolution fusion | flops 1614872576 | bytes 8945668 | tf_op jit(solution)/shard_map/while/body/eval_jaxpr/dot_general | solution.py:47
  148.6 3.4 multiply_bitcast_fusion
  152.0 2.0 copy.65
  154.0 9.3 %all-to-all-start = ((f32[128,8,512]{2,1,0:T(8,128)}), f32[128,8,512]{2,1,0:T(8,128)}, u32[]{:S(2)}, u32[]{:S(2)}) async-start(f32[128,8,512]{2,1,0:T(8,128)} %copy.65), calls=%async_computation | async-start | bytes 4194304 | tf_op jit(solution)/shard_map/all_to_all | solution.py:83
  163.5 28.7 %all-to-all-done = f32[128,8,512]{2,1,0:T(8,128)} async-done(((f32[128,8,512]{2,1,0:T(8,128)}), f32[128,8,512]{2,1,0:T(8,128)}, u32[]{:S(2)}, u32[]{:S(2)}) %all-to-all-start) | async-done | bytes 2097184 | tf_op jit(solution)/shard_map/all_to_all | solution.py:83
  192.2 2.3 broadcast_multiply_fusion
  198.0 4.2 %negate_exponential_fusion = f32[4,8,32,512]{3,2,1,0:T(8,128)} fusion(f32[32,4,8,512]{3,2,1,0:T(8,128)S(1)} %bitcast.70, f32[4,8,32]{2,1,0:T(8,128)S(1)} %sub.23), kind=kOutput, calls=%fused_computation.63 | convolution fusion | flops 3222536192 | bytes 4198400 | tf_op jit(solution)/shard_map/bkni,ij->bknj/dot_general | solution.py:89
  202.2 2.9 exp.7
  205.1 1.9 multiply_multiply_fusion
  207.0 3.2 fusion.56
  210.2 30.8 %copy.72 = f32[4,8,16384]{0,1,2:T(8,128)} copy(f32[4,8,16384]{2,0,1:T(4,128)S(1)} %fusion.56) | data formatting | bytes 4194304
  241.0 41.7 %reshape.39 = f32[16384,32]{1,0:T(8,128)} reshape(f32[16384,8,4]{2,1,0:T(8,128)} %bitcast.19) | data formatting | bytes 4194304
  282.7 1.6 copy-done.2
  284.3 2.0 copy.63
  286.2 96.8 %reduce-scatter.4.cloned.1.call-done = f32[512,32]{1,0:T(8,128)} async-done(((f32[16384,32]{1,0:T(8,128)}), f32[512,32]{1,0:T(8,128)}) %reduce-scatter.4.cloned.1.call-update) | async-done | bytes 65552
  383.0 1.6 reshape.40
  (32 shorter events, 6.4 us)
Async XLA Ops:
  7.2 141.4 %copy-start = (f32[128,128]{1,0:T(8,128)S(1)}, f32[128,128]{1,0:T(8,128)}, u32[]{:S(2)}) copy-start(f32[128,128]{1,0:T(8,128)} %param.15) | copy-start | bytes 196612
  9.2 12.1 %copy-start.4 = (s32[3,2048]{1,0:T(4,128)S(1)}, s32[3,2048]{1,0:T(4,128)}, u32[]{:S(2)}) copy-start(s32[3,2048]{1,0:T(4,128)} %param.13) | copy-start | bytes 73732
  9.2 18.1 %copy-start.5 = (f32[128]{0:T(128)S(1)}, f32[128]{0:T(128)}, u32[]{:S(2)}) copy-start(f32[128]{0:T(128)} %param.12) | copy-start | bytes 1540
  9.2 18.1 %copy-start.6 = (f32[128]{0:T(128)S(1)}, f32[128]{0:T(128)}, u32[]{:S(2)}) copy-start(f32[128]{0:T(128)} %param.11) | copy-start | bytes 1540
  9.3 3.1 collective-permute-start.1
  11.0 4.4 %collective-permute-start = (f32[128,8,1]{0,2,1:T(1,128)S(1)}, f32[128,8,1]{0,2,1:T(1,128)S(1)}, u32[]{:S(2)}, u32[]{:S(2)}) collective-permute-start(f32[128,8,1]{0,2,1:T(1,128)S(1)} %get-tuple-element.116), channel_id=1, source_target_pairs={{8,0},{16,8},{24,16},{32,24},{40,32},{48,40},{56,48},{64,56},{72,6... | collective-permute-start | bytes 12296 | tf_op jit(solution)/shard_map/ppermute | solution.py:20
  15.5 9.6 %collective-permute-start.2 = (f32[128,1,514]{0,2,1:T(8,128)S(1)}, f32[128,1,514]{0,2,1:T(8,128)S(1)}, u32[]{:S(2)}, u32[]{:S(2)}) collective-permute-start(f32[128,1,514]{0,2,1:T(8,128)S(1)} %get-tuple-element.111), channel_id=1, source_target_pairs={{1,0},{2,1},{3,2},{4,3},{5,4},{6,5},{7,6},{9,8},{10,9},{11,10},{12... | collective-permute-start | bytes 789512 | tf_op jit(solution)/shard_map/ppermute | solution.py:20
  17.5 9.9 %collective-permute-start.3 = (f32[128,1,514]{0,2,1:T(8,128)S(1)}, f32[128,1,514]{0,2,1:T(8,128)S(1)}, u32[]{:S(2)}, u32[]{:S(2)}) collective-permute-start(f32[128,1,514]{0,2,1:T(8,128)S(1)} %get-tuple-element.112), channel_id=1, source_target_pairs={{0,1},{1,2},{2,3},{3,4},{4,5},{5,6},{6,7},{8,9},{9,10},{10,11},{11... | collective-permute-start | bytes 789512 | tf_op jit(solution)/shard_map/ppermute | solution.py:18
  21.4 9.2 %copy-start.3 = (f32[2048]{0:T(1024)S(1)}, f32[2048]{0:T(1024)}, u32[]{:S(2)}) copy-start(f32[2048]{0:T(1024)} %param.14) | copy-start | bytes 24580
  154.0 9.4 %copy-start.7 = (f32[128]{0:T(128)S(1)}, f32[128]{0:T(128)}, u32[]{:S(2)}) copy-start(f32[128]{0:T(128)} %param.16) | copy-start | bytes 1540
  154.0 9.5 %copy-start.8 = (s32[128]{0:T(128)S(1)}, s32[128]{0:T(128)}, u32[]{:S(2)}) copy-start(s32[128]{0:T(128)} %param.17) | copy-start | bytes 1540
  154.0 38.2 %all-to-all-start = ((f32[128,8,512]{2,1,0:T(8,128)}), f32[128,8,512]{2,1,0:T(8,128)}, u32[]{:S(2)}, u32[]{:S(2)}) async-start(f32[128,8,512]{2,1,0:T(8,128)} %copy.65), calls=%async_computation | async-start | bytes 4194304 | tf_op jit(solution)/shard_map/all_to_all | solution.py:83
  163.3 219.7 %reduce-scatter.4.cloned.1.call-start = ((), (), s32[]{:S(2)}) async-start(), calls=%async_computation.2 | async-start | bytes 8650752
  202.2 2.9 copy-start.1
  282.7 1.6 copy-start.2
Sparse Core Ops, SparseCore 0:
  282.8 100.1 reduce-scatter.3
where the time goes:
time: 395 us; the launch traced here: 393 us
  waiting for transfers between devices  135 us (34%)
  matrix products  129 us (33%)
  local copies, waits for them, and re-layouts  87.7 us (22%)
  starting transfers between devices  18.2 us (5%)
  between operations  14.2 us (4%)
  other arithmetic  9.31 us (2%)
    unnamed x2, waiting for transfers between devices  96.8 us
    unnamed x23, local copies, waits for them, and re-layouts  79.1 us
    dot_general x8, matrix products, one_row(): jnp.dot(redistribute, product, precision=lax.Precision.HIGHEST, preferred...  44.4 us
    dot_general x8, matrix products, one_row(): jnp.dot(pick_first, column, precision=lax.Precision.HIGHEST, preferred_el...  36.8 us
    dot_general x8, matrix products, one_row(): jnp.dot(pick_second, column, precision=lax.Precision.HIGHEST, preferred_e...  36.7 us
    all_to_all x1, waiting for transfers between devices, shards(): lax.all_to_all(opacity, 'rad', split_axis=0, concat_axis=2, tiled=True)  28.7 us
    all_to_all x1, starting transfers between devices, shards(): lax.all_to_all(opacity, 'rad', split_axis=0, concat_axis=2, tiled=True)  9.3 us
  transfers between devices with their start and end apart: 6, of which 5 were waited for; matrix products, arithmetic and copies ran while one was open for 1% of the time, Pallas kernels for 0%

commit v1 on v0

--- a/solution.py
+++ b/solution.py
@@ -80,7 +80,15 @@
     cell_index = jnp.arange(tile, dtype=jnp.int32)
     strict_upper = (cell_index[:, None] < cell_index[None, :]).astype(jnp.float32)
     channels = jnp.arange(CH, dtype=jnp.int32)
-    ray_block = lax.all_to_all(opacity, "rad", split_axis=0, concat_axis=2, tiled=True)
+    ray_block = jnp.concatenate(
+        lax.all_to_all(
+            jnp.stack(jnp.split(opacity, lax.axis_size("rad"), 0)),
+            "rad",
+            concat_axis=0,
+            split_axis=0,
+        ),
+        2,
+    )
     local_bands = ray_block.shape[0]
     polar_rows = ray_block.shape[1]
     first_band = lax.axis_index("rad") * local_bands

time: 395 us -> 417 us (1.056)
  local copies, waits for them, and re-layouts: 87.7 us -> 110 us
    unnamed x23 -> x56, local copies, waits for them, and re-layouts: 79.1 us -> 98.6 us
where the time goes in v1:
time: 417 us; the launch traced here: 415 us
  waiting for transfers between devices  135 us (32%)
  matrix products  129 us (31%)
  local copies, waits for them, and re-layouts  110 us (26%)
  starting transfers between devices  18.1 us (4%)
  between operations  14.2 us (3%)
  other arithmetic  9.09 us (2%)
    unnamed x56, local copies, waits for them, and re-layouts  98.6 us
    unnamed x2, waiting for transfers between devices  96.8 us
    dot_general x8, matrix products, one_row(): jnp.dot(redistribute, product, precision=lax.Precision.HIGHEST, preferred...  44.4 us
    dot_general x8, matrix products, one_row(): jnp.dot(pick_first, column, precision=lax.Precision.HIGHEST, preferred_el...  36.8 us
    dot_general x8, matrix products, one_row(): jnp.dot(pick_second, column, precision=lax.Precision.HIGHEST, preferred_e...  36.7 us
    all_to_all x1, waiting for transfers between devices, shards(): lax.all_to_all(jnp.stack(jnp.split(opacity, lax.axis_size('rad'), 0)), 'r...  28.7 us
    all_to_all x1, starting transfers between devices, shards(): lax.all_to_all(jnp.stack(jnp.split(opacity, lax.axis_size('rad'), 0)), 'r...  9.17 us
  transfers between devices with their start and end apart: 6, of which 5 were waited for; matrix products, arithmetic and copies ran while one was open for 1% of the time, Pallas kernels for 0%

profile of v1, /device:TPU:32, one launch (start us, length us, event | category | flops | bytes accessed | tf_op | source)
XLA Modules:
  0.0 414.9 jit_solution(971978626956984667)
XLA Ops:
  7.2 2.0 copy.40
  9.3 1.7 collective-permute-start.1
  12.3 3.1 collective-permute-done
  15.5 2.0 collective-permute-start.2
  17.5 3.8 collective-permute-start.3
  21.4 3.7 collective-permute-done.2
  25.1 2.3 collective-permute-done.3
  27.4 3.1 fusion.46
  30.5 118.0 %while.12 = (s32[]{:T(128)}, f32[8,128,512]{1,2,0:T(8,128)}, f32[8,128,512]{1,2,0:T(8,128)}, f32[2048]{0:T(1024)S(1)}, s32[2048]{0:T(1024)S(1)}, /*index=5*/s32[2048]{0:T(1024)S(1)}, s32[2048]{0:T(1024)S(1)}, s32[]{:T(128)}) while((s32[]{:T(128)}, f32[8,128,512]{1,2,0:T(8,128)}, f32[8,128,512]{1,2,0:T(8,128)}, ...), condition=%wide.region_1.2_spmd.clone.clone, body=%wide.region_0.1_spmd.clone.clone.sunk | while | flops 4837146624 | bytes 17875048 | solution.py:54
  30.5 4.6 %fusion.86 = f32[512,2048]{1,0:T(8,128)S(1)} fusion(s32[2048]{0:T(1024)S(1)} %get-tuple-element.182, f32[8,128,512]{1,2,0:T(8,128)} %get-tuple-element.179, s32[]{:T(128)S(6)} %copy.67), kind=kOutput, calls=%fused_computation.19.clone.1 | convolution fusion | flops 1611137024 | bytes 4464644 | tf_op jit(solution)/shard_map/while/body/eval_jaxpr/dot_general | solution.py:43
  35.1 4.6 %fusion.87 = f32[512,2048]{1,0:T(8,128)S(1)} fusion(s32[2048]{0:T(1024)S(1)} %get-tuple-element.181, f32[8,128,512]{1,2,0:T(8,128)} %get-tuple-element.179, s32[]{:T(128)S(6)} %copy.67), kind=kOutput, calls=%fused_computation.22.clone.1 | convolution fusion | flops 1611137024 | bytes 4464644 | tf_op jit(solution)/shard_map/while/body/eval_jaxpr/dot_general | solution.py:40
  39.7 5.6 %fusion.88 = f32[8,128,512]{1,2,0:T(8,128)} fusion(f32[8,128,512]{1,2,0:T(8,128)} %get-tuple-element.170, s32[]{:T(128)S(6)} %copy.67, f32[512,2048]{1,0:T(8,128)S(1)} %fusion.86, f32[512,2048]{1,0:T(8,128)S(1)} %fusion.87, f32[2048]{0:T(1024)S(1)} %get-tuple-element.180, s32[2048]{0:T(1024)S(1)} %get-tuple-element.182, ...), kind=kOutput, calls=%fused_computation.10.clone.1 | convolution fusion | flops 1614872576 | bytes 8945668 | tf_op jit(solution)/shard_map/while/body/eval_jaxpr/dot_general | solution.py:47
  45.2 4.6 %fusion.86 = f32[512,2048]{1,0:T(8,128)S(1)} fusion(s32[2048]{0:T(1024)S(1)} %get-tuple-element.182, f32[8,128,512]{1,2,0:T(8,128)} %get-tuple-element.179, s32[]{:T(128)S(6)} %copy.67), kind=kOutput, calls=%fused_computation.19.clone.1 | convolution fusion | flops 1611137024 | bytes 4464644 | tf_op jit(solution)/shard_map/while/body/eval_jaxpr/dot_general | solution.py:43
  49.8 4.6 %fusion.87 = f32[512,2048]{1,0:T(8,128)S(1)} fusion(s32[2048]{0:T(1024)S(1)} %get-tuple-element.181, f32[8,128,512]{1,2,0:T(8,128)} %get-tuple-element.179, s32[]{:T(128)S(6)} %copy.67), kind=kOutput, calls=%fused_computation.22.clone.1 | convolution fusion | flops 1611137024 | bytes 4464644 | tf_op jit(solution)/shard_map/while/body/eval_jaxpr/dot_general | solution.py:40
  54.4 5.6 %fusion.88 = f32[8,128,512]{1,2,0:T(8,128)} fusion(f32[8,128,512]{1,2,0:T(8,128)} %get-tuple-element.170, s32[]{:T(128)S(6)} %copy.67, f32[512,2048]{1,0:T(8,128)S(1)} %fusion.86, f32[512,2048]{1,0:T(8,128)S(1)} %fusion.87, f32[2048]{0:T(1024)S(1)} %get-tuple-element.180, s32[2048]{0:T(1024)S(1)} %get-tuple-element.182, ...), kind=kOutput, calls=%fused_computation.10.clone.1 | convolution fusion | flops 1614872576 | bytes 8945668 | tf_op jit(solution)/shard_map/while/body/eval_jaxpr/dot_general | solution.py:47
  60.0 4.6 %fusion.86 = f32[512,2048]{1,0:T(8,128)S(1)} fusion(s32[2048]{0:T(1024)S(1)} %get-tuple-element.182, f32[8,128,512]{1,2,0:T(8,128)} %get-tuple-element.179, s32[]{:T(128)S(6)} %copy.67), kind=kOutput, calls=%fused_computation.19.clone.1 | convolution fusion | flops 1611137024 | bytes 4464644 | tf_op jit(solution)/shard_map/while/body/eval_jaxpr/dot_general | solution.py:43
  64.6 4.6 %fusion.87 = f32[512,2048]{1,0:T(8,128)S(1)} fusion(s32[2048]{0:T(1024)S(1)} %get-tuple-element.181, f32[8,128,512]{1,2,0:T(8,128)} %get-tuple-element.179, s32[]{:T(128)S(6)} %copy.67), kind=kOutput, calls=%fused_computation.22.clone.1 | convolution fusion | flops 1611137024 | bytes 4464644 | tf_op jit(solution)/shard_map/while/body/eval_jaxpr/dot_general | solution.py:40
  69.2 5.6 %fusion.88 = f32[8,128,512]{1,2,0:T(8,128)} fusion(f32[8,128,512]{1,2,0:T(8,128)} %get-tuple-element.170, s32[]{:T(128)S(6)} %copy.67, f32[512,2048]{1,0:T(8,128)S(1)} %fusion.86, f32[512,2048]{1,0:T(8,128)S(1)} %fusion.87, f32[2048]{0:T(1024)S(1)} %get-tuple-element.180, s32[2048]{0:T(1024)S(1)} %get-tuple-element.182, ...), kind=kOutput, calls=%fused_computation.10.clone.1 | convolution fusion | flops 1614872576 | bytes 8945668 | tf_op jit(solution)/shard_map/while/body/eval_jaxpr/dot_general | solution.py:47
  74.7 4.6 %fusion.86 = f32[512,2048]{1,0:T(8,128)S(1)} fusion(s32[2048]{0:T(1024)S(1)} %get-tuple-element.182, f32[8,128,512]{1,2,0:T(8,128)} %get-tuple-element.179, s32[]{:T(128)S(6)} %copy.67), kind=kOutput, calls=%fused_computation.19.clone.1 | convolution fusion | flops 1611137024 | bytes 4464644 | tf_op jit(solution)/shard_map/while/body/eval_jaxpr/dot_general | solution.py:43
  79.3 4.6 %fusion.87 = f32[512,2048]{1,0:T(8,128)S(1)} fusion(s32[2048]{0:T(1024)S(1)} %get-tuple-element.181, f32[8,128,512]{1,2,0:T(8,128)} %get-tuple-element.179, s32[]{:T(128)S(6)} %copy.67), kind=kOutput, calls=%fused_computation.22.clone.1 | convolution fusion | flops 1611137024 | bytes 4464644 | tf_op jit(solution)/shard_map/while/body/eval_jaxpr/dot_general | solution.py:40
  83.9 5.6 %fusion.88 = f32[8,128,512]{1,2,0:T(8,128)} fusion(f32[8,128,512]{1,2,0:T(8,128)} %get-tuple-element.170, s32[]{:T(128)S(6)} %copy.67, f32[512,2048]{1,0:T(8,128)S(1)} %fusion.86, f32[512,2048]{1,0:T(8,128)S(1)} %fusion.87, f32[2048]{0:T(1024)S(1)} %get-tuple-element.180, s32[2048]{0:T(1024)S(1)} %get-tuple-element.182, ...), kind=kOutput, calls=%fused_computation.10.clone.1 | convolution fusion | flops 1614872576 | bytes 8945668 | tf_op jit(solution)/shard_map/while/body/eval_jaxpr/dot_general | solution.py:47
  89.5 4.6 %fusion.86 = f32[512,2048]{1,0:T(8,128)S(1)} fusion(s32[2048]{0:T(1024)S(1)} %get-tuple-element.182, f32[8,128,512]{1,2,0:T(8,128)} %get-tuple-element.179, s32[]{:T(128)S(6)} %copy.67), kind=kOutput, calls=%fused_computation.19.clone.1 | convolution fusion | flops 1611137024 | bytes 4464644 | tf_op jit(solution)/shard_map/while/body/eval_jaxpr/dot_general | solution.py:43
  94.1 4.6 %fusion.87 = f32[512,2048]{1,0:T(8,128)S(1)} fusion(s32[2048]{0:T(1024)S(1)} %get-tuple-element.181, f32[8,128,512]{1,2,0:T(8,128)} %get-tuple-element.179, s32[]{:T(128)S(6)} %copy.67), kind=kOutput, calls=%fused_computation.22.clone.1 | convolution fusion | flops 1611137024 | bytes 4464644 | tf_op jit(solution)/shard_map/while/body/eval_jaxpr/dot_general | solution.py:40
  98.7 5.6 %fusion.88 = f32[8,128,512]{1,2,0:T(8,128)} fusion(f32[8,128,512]{1,2,0:T(8,128)} %get-tuple-element.170, s32[]{:T(128)S(6)} %copy.67, f32[512,2048]{1,0:T(8,128)S(1)} %fusion.86, f32[512,2048]{1,0:T(8,128)S(1)} %fusion.87, f32[2048]{0:T(1024)S(1)} %get-tuple-element.180, s32[2048]{0:T(1024)S(1)} %get-tuple-element.182, ...), kind=kOutput, calls=%fused_computation.10.clone.1 | convolution fusion | flops 1614872576 | bytes 8945668 | tf_op jit(solution)/shard_map/while/body/eval_jaxpr/dot_general | solution.py:47
  104.3 4.6 %fusion.86 = f32[512,2048]{1,0:T(8,128)S(1)} fusion(s32[2048]{0:T(1024)S(1)} %get-tuple-element.182, f32[8,128,512]{1,2,0:T(8,128)} %get-tuple-element.179, s32[]{:T(128)S(6)} %copy.67), kind=kOutput, calls=%fused_computation.19.clone.1 | convolution fusion | flops 1611137024 | bytes 4464644 | tf_op jit(solution)/shard_map/while/body/eval_jaxpr/dot_general | solution.py:43
  108.9 4.6 %fusion.87 = f32[512,2048]{1,0:T(8,128)S(1)} fusion(s32[2048]{0:T(1024)S(1)} %get-tuple-element.181, f32[8,128,512]{1,2,0:T(8,128)} %get-tuple-element.179, s32[]{:T(128)S(6)} %copy.67), kind=kOutput, calls=%fused_computation.22.clone.1 | convolution fusion | flops 1611137024 | bytes 4464644 | tf_op jit(solution)/shard_map/while/body/eval_jaxpr/dot_general | solution.py:40
  113.5 5.6 %fusion.88 = f32[8,128,512]{1,2,0:T(8,128)} fusion(f32[8,128,512]{1,2,0:T(8,128)} %get-tuple-element.170, s32[]{:T(128)S(6)} %copy.67, f32[512,2048]{1,0:T(8,128)S(1)} %fusion.86, f32[512,2048]{1,0:T(8,128)S(1)} %fusion.87, f32[2048]{0:T(1024)S(1)} %get-tuple-element.180, s32[2048]{0:T(1024)S(1)} %get-tuple-element.182, ...), kind=kOutput, calls=%fused_computation.10.clone.1 | convolution fusion | flops 1614872576 | bytes 8945668 | tf_op jit(solution)/shard_map/while/body/eval_jaxpr/dot_general | solution.py:47
  119.0 4.6 %fusion.86 = f32[512,2048]{1,0:T(8,128)S(1)} fusion(s32[2048]{0:T(1024)S(1)} %get-tuple-element.182, f32[8,128,512]{1,2,0:T(8,128)} %get-tuple-element.179, s32[]{:T(128)S(6)} %copy.67), kind=kOutput, calls=%fused_computation.19.clone.1 | convolution fusion | flops 1611137024 | bytes 4464644 | tf_op jit(solution)/shard_map/while/body/eval_jaxpr/dot_general | solution.py:43
  123.6 4.6 %fusion.87 = f32[512,2048]{1,0:T(8,128)S(1)} fusion(s32[2048]{0:T(1024)S(1)} %get-tuple-element.181, f32[8,128,512]{1,2,0:T(8,128)} %get-tuple-element.179, s32[]{:T(128)S(6)} %copy.67), kind=kOutput, calls=%fused_computation.22.clone.1 | convolution fusion | flops 1611137024 | bytes 4464644 | tf_op jit(solution)/shard_map/while/body/eval_jaxpr/dot_general | solution.py:40
  128.2 5.6 %fusion.88 = f32[8,128,512]{1,2,0:T(8,128)} fusion(f32[8,128,512]{1,2,0:T(8,128)} %get-tuple-element.170, s32[]{:T(128)S(6)} %copy.67, f32[512,2048]{1,0:T(8,128)S(1)} %fusion.86, f32[512,2048]{1,0:T(8,128)S(1)} %fusion.87, f32[2048]{0:T(1024)S(1)} %get-tuple-element.180, s32[2048]{0:T(1024)S(1)} %get-tuple-element.182, ...), kind=kOutput, calls=%fused_computation.10.clone.1 | convolution fusion | flops 1614872576 | bytes 8945668 | tf_op jit(solution)/shard_map/while/body/eval_jaxpr/dot_general | solution.py:47
  133.8 4.6 %fusion.86 = f32[512,2048]{1,0:T(8,128)S(1)} fusion(s32[2048]{0:T(1024)S(1)} %get-tuple-element.182, f32[8,128,512]{1,2,0:T(8,128)} %get-tuple-element.179, s32[]{:T(128)S(6)} %copy.67), kind=kOutput, calls=%fused_computation.19.clone.1 | convolution fusion | flops 1611137024 | bytes 4464644 | tf_op jit(solution)/shard_map/while/body/eval_jaxpr/dot_general | solution.py:43
  138.4 4.6 %fusion.87 = f32[512,2048]{1,0:T(8,128)S(1)} fusion(s32[2048]{0:T(1024)S(1)} %get-tuple-element.181, f32[8,128,512]{1,2,0:T(8,128)} %get-tuple-element.179, s32[]{:T(128)S(6)} %copy.67), kind=kOutput, calls=%fused_computation.22.clone.1 | convolution fusion | flops 1611137024 | bytes 4464644 | tf_op jit(solution)/shard_map/while/body/eval_jaxpr/dot_general | solution.py:40
  143.0 5.6 %fusion.88 = f32[8,128,512]{1,2,0:T(8,128)} fusion(f32[8,128,512]{1,2,0:T(8,128)} %get-tuple-element.170, s32[]{:T(128)S(6)} %copy.67, f32[512,2048]{1,0:T(8,128)S(1)} %fusion.86, f32[512,2048]{1,0:T(8,128)S(1)} %fusion.87, f32[2048]{0:T(1024)S(1)} %get-tuple-element.180, s32[2048]{0:T(1024)S(1)} %get-tuple-element.182, ...), kind=kOutput, calls=%fused_computation.10.clone.1 | convolution fusion | flops 1614872576 | bytes 8945668 | tf_op jit(solution)/shard_map/while/body/eval_jaxpr/dot_general | solution.py:47
  148.5 3.6 multiply_bitcast_fusion
  172.3 9.2 %all-to-all-start = ((f32[32,4,8,512]{3,1,2,0:T(4,128)}), f32[32,4,8,512]{3,1,2,0:T(4,128)S(1)}, u32[]{:S(2)}, u32[]{:S(2)}) async-start(f32[32,4,8,512]{3,1,2,0:T(4,128)} %constant_dynamic-update-slice_fusion), calls=%async_computation | async-start | bytes 4194304 | tf_op jit(solution)/shard_map/all_to_all | solution.py:84
  181.7 28.7 %all-to-all-done = f32[32,4,8,512]{3,1,2,0:T(4,128)S(1)} async-done(((f32[32,4,8,512]{3,1,2,0:T(4,128)}), f32[32,4,8,512]{3,1,2,0:T(4,128)S(1)}, u32[]{:S(2)}, u32[]{:S(2)}) %all-to-all-start) | async-done | bytes 2097184 | tf_op jit(solution)/shard_map/all_to_all | solution.py:84
  211.8 2.8 multiply_bitcast_fusion.1
  214.6 4.2 %negate_exponential_fusion = f32[4,8,32,512]{3,2,1,0:T(8,128)} fusion(f32[4,8,32,512]{3,0,1,2:T(4,128)S(1)} %get-tuple-element.111, f32[4,8,32]{2,1,0:T(8,128)S(1)} %sub.23), kind=kOutput, calls=%fused_computation.62 | convolution fusion | flops 3222536192 | bytes 4198400 | tf_op jit(solution)/shard_map/bkni,ij->bknj/dot_general | solution.py:97
  218.8 2.9 exp.7
  221.7 2.6 copy.50
  224.3 2.9 neg.18
  227.2 1.9 multiply_multiply_fusion
  229.0 3.2 fusion.54
  232.3 30.8 %copy.55 = f32[4,8,16384]{0,1,2:T(8,128)} copy(f32[4,8,16384]{2,0,1:T(4,128)S(1)} %fusion.54) | data formatting | bytes 4194304
  263.1 41.7 %reshape.34 = f32[16384,32]{1,0:T(8,128)} reshape(f32[16384,8,4]{2,1,0:T(8,128)} %bitcast.49) | data formatting | bytes 4194304
  306.3 2.0 copy.45
  308.3 96.8 %reduce-scatter.4.cloned.1.call-done = f32[512,32]{1,0:T(8,128)} async-done(((f32[16384,32]{1,0:T(8,128)}), f32[512,32]{1,0:T(8,128)}) %reduce-scatter.4.cloned.1.call-update) | async-done | bytes 65552
  405.0 1.6 reshape.35
  (67 shorter events, 26.1 us)
Async XLA Ops:
  7.2 141.4 %copy-start = (f32[128,128]{1,0:T(8,128)S(1)}, f32[128,128]{1,0:T(8,128)}, u32[]{:S(2)}) copy-start(f32[128,128]{1,0:T(8,128)} %param.15) | copy-start | bytes 196612
  9.2 12.1 %copy-start.5 = (s32[3,2048]{1,0:T(4,128)S(1)}, s32[3,2048]{1,0:T(4,128)}, u32[]{:S(2)}) copy-start(s32[3,2048]{1,0:T(4,128)} %param.13) | copy-start | bytes 73732
  9.2 18.1 %copy-start.6 = (f32[128]{0:T(128)S(1)}, f32[128]{0:T(128)}, u32[]{:S(2)}) copy-start(f32[128]{0:T(128)} %param.12) | copy-start | bytes 1540
  9.2 18.1 %copy-start.7 = (f32[128]{0:T(128)S(1)}, f32[128]{0:T(128)}, u32[]{:S(2)}) copy-start(f32[128]{0:T(128)} %param.11) | copy-start | bytes 1540
  9.3 3.1 collective-permute-start.1
  11.0 4.4 %collective-permute-start = (f32[128,8,1]{0,2,1:T(1,128)S(1)}, f32[128,8,1]{0,2,1:T(1,128)S(1)}, u32[]{:S(2)}, u32[]{:S(2)}) collective-permute-start(f32[128,8,1]{0,2,1:T(1,128)S(1)} %get-tuple-element.114), channel_id=1, source_target_pairs={{8,0},{16,8},{24,16},{32,24},{40,32},{48,40},{56,48},{64,56},{72,6... | collective-permute-start | bytes 12296 | tf_op jit(solution)/shard_map/ppermute | solution.py:20
  15.5 9.6 %collective-permute-start.2 = (f32[128,1,514]{0,2,1:T(8,128)S(1)}, f32[128,1,514]{0,2,1:T(8,128)S(1)}, u32[]{:S(2)}, u32[]{:S(2)}) collective-permute-start(f32[128,1,514]{0,2,1:T(8,128)S(1)} %get-tuple-element.109), channel_id=1, source_target_pairs={{1,0},{2,1},{3,2},{4,3},{5,4},{6,5},{7,6},{9,8},{10,9},{11,10},{12... | collective-permute-start | bytes 789512 | tf_op jit(solution)/shard_map/ppermute | solution.py:20
  17.5 9.9 %collective-permute-start.3 = (f32[128,1,514]{0,2,1:T(8,128)S(1)}, f32[128,1,514]{0,2,1:T(8,128)S(1)}, u32[]{:S(2)}, u32[]{:S(2)}) collective-permute-start(f32[128,1,514]{0,2,1:T(8,128)S(1)} %get-tuple-element.110), channel_id=1, source_target_pairs={{0,1},{1,2},{2,3},{3,4},{4,5},{5,6},{6,7},{8,9},{9,10},{10,11},{11... | collective-permute-start | bytes 789512 | tf_op jit(solution)/shard_map/ppermute | solution.py:18
  21.4 9.1 %copy-start.4 = (f32[2048]{0:T(1024)S(1)}, f32[2048]{0:T(1024)}, u32[]{:S(2)}) copy-start(f32[2048]{0:T(1024)} %param.14) | copy-start | bytes 24580
  172.3 9.2 %copy-start.8 = (f32[128]{0:T(128)S(1)}, f32[128]{0:T(128)}, u32[]{:S(2)}) copy-start(f32[128]{0:T(128)} %param.16) | copy-start | bytes 1540
  172.3 9.3 %copy-start.9 = (s32[128]{0:T(128)S(1)}, s32[128]{0:T(128)}, u32[]{:S(2)}) copy-start(s32[128]{0:T(128)} %param.17) | copy-start | bytes 1540
  172.3 38.1 %all-to-all-start = ((f32[32,4,8,512]{3,1,2,0:T(4,128)}), f32[32,4,8,512]{3,1,2,0:T(4,128)S(1)}, u32[]{:S(2)}, u32[]{:S(2)}) async-start(f32[32,4,8,512]{3,1,2,0:T(4,128)} %constant_dynamic-update-slice_fusion), calls=%async_computation | async-start | bytes 4194304 | tf_op jit(solution)/shard_map/all_to_all | solution.py:84
  181.5 223.6 %reduce-scatter.4.cloned.1.call-start = ((), (), s32[]{:S(2)}) async-start(), calls=%async_computation.2 | async-start | bytes 8650752
  218.8 2.9 copy-start.1
  224.3 2.9 copy-start.2
  304.7 1.6 copy-start.3
Sparse Core Ops, SparseCore 0:
  304.9 100.1 reduce-scatter.3
